TPU v7x, 256 devices: a whole 4x4x8 slice. The times are simulated.
256 devices in a mesh: az: 64 (over x, y_hi, z), ax: 4 (over y_lo, core).
Axes of the slice: x: 4, y: 4 (y_hi: 2, y_lo: 2; y = y_hi * 2 + y_lo), z: 8, core: 2. Of those that a mesh axis runs over, the one named last changes fastest.
Arguments:
- fields: float32 [5, 64, 1024, 512], P(None, 'ax', 'az'), may hold values from -6.5 to 6.5, as said below
Outputs:
- advanced: float32 [5, 64, 1024, 512], P(None, 'ax', 'az')
Inputs may be any that keep to these rules, and one draw needn't show every extreme that they name: `fields`: each field is a rough part plus, on every axial plane and cycle, a constant and a first azimuthal harmonic.
All inputs are finite; a program needn't handle non-finite values.
Results may differ from a plain program's by a relative error of at most 0.0003.
Values sent between devices are 32-bit elements; how exact they have to be, the bound alone decides.
A program may use at most 128 MiB of HBM per device.

v0:
```python
import jax
import jax.numpy as jnp
from jax import lax
from jax.sharding import PartitionSpec as P

NEAR = 40
viscosity = 0.2
time_step = 0.1
buoyancy = 1.0


def swapped(block, axis, distance):
    count = lax.axis_size(axis)
    route = []
    for low in range(count):
        high = low | 1 << distance
        if high != low and high < count:
            route += [(low, high), (high, low)]
    return lax.ppermute(block, axis, route)


def with_halo(block, sides, width, periodic):
    for axis, dim in sides:
        count = lax.axis_size(axis)
        forward = [(i, i + 1) for i in range(count - 1)]
        if periodic:
            forward.append((count - 1, 0))
        backward = [(target, source) for source, target in forward]
        low = lax.ppermute(
            lax.slice_in_dim(block, block.shape[dim] - width, None, axis=dim), axis, forward
        )
        high = lax.ppermute(lax.slice_in_dim(block, 0, width, axis=dim), axis, backward)
        block = jnp.concatenate([low, block, high], axis=dim)
    return block


def mode_tables(theta_index, total_theta, modes):
    column = jnp.arange(modes, dtype=jnp.int32)
    product = theta_index[:, None] * column[None, :] % total_theta
    angle = product.astype(jnp.float32) * (2.0 * jnp.pi / total_theta)
    cosine = jnp.cos(angle)
    sine = jnp.sin(angle)
    weight = jnp.where(column == 0, 1.0, 2.0).astype(jnp.float32) / total_theta
    forward = jnp.concatenate([cosine * weight[None, :], sine * (2.0 / total_theta)], axis=1)
    inverse = jnp.concatenate([cosine, sine], axis=1)
    return (forward, inverse)


def cycle_mask(cycles, modes):
    cycle_index = jnp.arange(cycles, dtype=jnp.int32)
    cutoff = jnp.minimum(355 * (2 * cycle_index + 1) // 226, modes - 1)
    column = jnp.arange(modes, dtype=jnp.int32)
    keep = (column[None, :] <= cutoff[:, None]).astype(jnp.float32)
    return jnp.concatenate([keep, keep], axis=1)


def operators(
    center, radial_plus, radial_minus, theta_plus, theta_minus, axial_plus, axial_minus, total_theta
):
    radius = jnp.arange(center.shape[-1], dtype=jnp.float32) + 0.5
    step_angle = 2.0 * jnp.pi / total_theta
    d_radial = (radial_plus - radial_minus) * 0.5
    d_theta = (theta_plus - theta_minus) / (2.0 * step_angle)
    d_axial = (axial_plus - axial_minus) * 0.5
    laplace = (
        radial_plus - 2.0 * center + radial_minus + (radial_plus - radial_minus) / (2.0 * radius)
    )
    laplace = laplace + (theta_plus - 2.0 * center + theta_minus) / (
        radius * radius * step_angle * step_angle
    )
    laplace = laplace + axial_plus - 2.0 * center + axial_minus
    return (d_radial, d_theta, d_axial, laplace)


def on_device(fields):
    count_fields, planes, theta_dev, radial = fields.shape
    sectors = lax.axis_size("az")
    total_theta = theta_dev * sectors
    modes = min(128, total_theta // 2)
    sector = lax.axis_index("az")
    own_index = sector * theta_dev + jnp.arange(theta_dev, dtype=jnp.int32)
    own_forward, own_inverse = mode_tables(own_index, total_theta, modes)
    inner_cycles = fields[:, :, :, :NEAR]
    kept = None
    piece = lax.all_gather(inner_cycles, "az", axis=2, tiled=True)
    piece_index = jnp.arange(piece.shape[2], dtype=jnp.int32)
    piece_forward, unused_inverse = mode_tables(piece_index, total_theta, modes)
    spectra = jnp.einsum("fztj,tc->fzjc", piece, piece_forward, precision=lax.Precision.HIGHEST)
    kept = spectra * cycle_mask(NEAR, modes)[None, None]
    smoothed = jnp.einsum("fzjc,tc->fztj", kept, own_inverse, precision=lax.Precision.HIGHEST)
    state = jnp.concatenate([smoothed, fields[:, :, :, NEAR:]], axis=3)
    flip = jnp.array([-1.0, -1.0, 1.0, 1.0, 1.0], dtype=jnp.float32)[:, None, None]
    top_bit = sectors.bit_length() - 1
    opposite = swapped(state[:, :, :, 0], "az", top_bit - 1)
    opposite = opposite * flip
    theta_padded = with_halo(state, (("az", 2),), 1, True)
    axial_padded = with_halo(state, (("ax", 1),), 1, False)
    radial_plus = jnp.concatenate([state[:, :, :, 1:], jnp.zeros_like(state[:, :, :, :1])], axis=3)
    radial_minus = jnp.concatenate([opposite[:, :, :, None], state[:, :, :, :-1]], axis=3)
    d_radial, d_theta, d_axial, laplace = operators(
        state,
        radial_plus,
        radial_minus,
        theta_padded[:, :, 2:, :],
        theta_padded[:, :, :-2, :],
        axial_padded[:, 2:, :, :],
        axial_padded[:, :-2, :, :],
        total_theta,
    )
    radius = jnp.arange(radial, dtype=jnp.float32) + 0.5
    radial_u = state[0]
    theta_u = state[1]
    axial_u = state[2]
    change = (
        -(radial_u[None] * d_radial + (theta_u / radius)[None] * d_theta + axial_u[None] * d_axial)
        + viscosity * laplace
    )
    inverse_square = 1.0 / (radius * radius)
    first = (
        change[0]
        + theta_u * theta_u / radius
        - viscosity * (radial_u * inverse_square + 2.0 * inverse_square * d_theta[1])
    )
    second = (
        change[1]
        - radial_u * theta_u / radius
        - viscosity * (theta_u * inverse_square - 2.0 * inverse_square * d_theta[0])
    )
    third = change[2] + buoyancy * state[3]
    change = jnp.concatenate([first[None], second[None], third[None], change[3:]], axis=0)
    return state + time_step * change


def solution(mesh):
    placed = (P(None, "ax", "az", None),)
    return jax.shard_map(
        on_device, mesh=mesh, in_specs=placed, out_specs=P(None, "ax", "az", None), check_vma=False
    )
```

profile of v0, /device:TPU:1, one launch (start us, length us, event | category | flops | bytes accessed | tf_op | source)
XLA Modules:
  0.0 499.4 jit_solution(17314941103463150801)
XLA Ops:
  6.5 0.0 all-gather.2.cloned.1.call-start
  6.5 2.0 slice.73
  8.5 0.0 all-gather.2.cloned.1.call-update
  8.6 4.0 slice.74
  12.5 3.2 copy.19
  15.9 0.1 iota_compare_fusion
  16.0 0.1 fusion.43
  16.1 3.0 sine_multiply_fusion
  19.1 355.6 %all-gather.2.cloned.1.call-done = f32[5,16,1024,40]{3,2,1,0:T(8,128)} async-done(((f32[5,16,16,40]{3,2,1,0:T(8,128)}), f32[5,16,1024,40]{3,2,1,0:T(8,128)}) %all-gather.2.cloned.1.call-update) | async-done | bytes 13107216 | tf_op jit(solution)/shard_map/all_gather | solution.py:85
  374.7 70.2 %fusion.8 = f32[256,5,16,40]{0,3,2,1:T(8,128)S(1)} fusion(f32[5,16,1024,40]{3,2,1,0:T(8,128)} %all-gather.2.cloned.1.call-done, f32[1024,128]{1,0:T(8,128)S(1)} %get-tuple-element.19, f32[1024,128]{1,0:T(8,128)} %get-tuple-element.20), kind=kOutput, calls=%fused_computation.40 | convolution fusion | flops 10066591744 | bytes 17432576 | tf_op jit(solution)/shard_map/fztj,tc->fzjc/dot_general | solution.py:88
  444.9 5.4 %fusion.7 = f32[5,16,16,40]{3,2,1,0:T(8,128)S(1)} fusion(f32[256,5,16,40]{0,3,2,1:T(8,128)S(1)} %fusion.8, f32[40,256]{1,0:T(8,128)S(1)} %add_convert_fusion, f32[16,128]{1,0:T(8,128)S(1)} %get-tuple-element.18, f32[16,128]{1,0:T(8,128)S(1)} %get-tuple-element.17), kind=kOutput, calls=%fused_computation.38 | convolution fusion | flops 158109696 | bytes 3538944 | tf_op jit(solution)/shard_map/fzjc,tc->fztj/dot_general | solution.py:90
  450.3 0.2 copy.10
  450.5 0.9 fusion.33
  451.4 3.9 fusion.1
  455.3 0.2 slice_reduce_fusion
  455.6 1.6 multiply_bitcast_fusion.1
  457.2 0.0 copy-start
  457.2 2.7 collective-permute-start
  459.9 0.7 fusion.31
  460.6 2.3 collective-permute-start.1
  462.9 0.0 collective-permute-start.2
  462.9 0.7 copy.12
  463.6 6.0 %collective-permute-start.3 = (f32[5,1,16,512]{3,2,1,0:T(8,128)}, f32[5,1,16,512]{3,2,1,0:T(8,128)}, u32[]{:S(2)}, u32[]{:S(2)}) collective-permute-start(f32[5,1,16,512]{3,2,1,0:T(8,128)} %copy.12), channel_id=1, source_target_pairs={{1,0},{2,1},{3,2},{5,4},{6,5},{7,6},{9,8},{10,9},{11,10},{13,12},{... | collective-permute-start | bytes 491528 | tf_op jit(solution)/shard_map/ppermute | solution.py:32
  469.6 0.7 copy.14
  470.2 3.0 collective-permute-start.4
  473.2 0.0 collective-permute-done
  473.3 0.0 copy-done
  473.3 0.1 multiply_bitcast_fusion.2
  473.3 1.4 copy.11
  474.7 1.3 collective-permute-done.3
  476.0 1.1 copy.13
  477.1 0.0 collective-permute-done.4
  477.1 1.1 copy.15
  478.2 0.0 collective-permute-done.1
  478.2 0.0 collective-permute-done.2
  478.2 7.4 %multiply_add_fusion = f32[5,16,16,512]{3,1,2,0:T(8,128)S(1)} fusion(f32[5,1,16,512]{3,1,2,0:T(1,128)S(1)} %copy.13, f32[5,16,16,472]{3,1,2,0:T(8,128)S(1)} %copy.19, f32[5,16,16,40]{3,1,2,0:T(8,128)S(1)} %copy.10, f32[5,1,16,512]{3,1,2,0:T(1,128)S(1)} %copy.15, f32[5,16,16,511]{3,1,2,0:T(8,128)} %get-tuple-element.14, f32[5,16,16,1]{3,1,2,0:T(8,128)} %copy.11, ...), kind=kLoop, calls=%fused_computation.26 | loop fusion | flops 21626880 | bytes 12712960 | tf_op jit(solution)/shard_map/add | solution.py:115
  485.6 0.1 slice.122
  485.7 2.3 fusion.6
  488.0 0.8 fusion.26
  488.8 0.8 fusion.3
  489.6 3.0 copy.16
  (7 shorter events, 0.1 us)
Async XLA Ops:
  6.5 368.2 %all-gather.2.cloned.1.call-start = ((), (), s32[]{:S(2)}) async-start(), calls=%async_computation | async-start | bytes 42598400 | tf_op jit(solution)/shard_map/all_gather | solution.py:85
  457.2 16.1 %copy-start = (f32[5]{0:T(128)S(1)}, f32[5]{0:T(128)}, u32[]{:S(2)}) copy-start(f32[5]{0:T(128)} %constant.82.clone) | copy-start | bytes 64
  457.2 16.1 %collective-permute-start = (f32[5,16,16]{2,1,0:T(8,128)S(1)}, f32[5,16,16]{2,1,0:T(8,128)S(1)}, u32[]{:S(2)}, u32[]{:S(2)}) collective-permute-start(f32[5,16,16]{2,1,0:T(8,128)S(1)} %slice_reduce_fusion), channel_id=1, source_target_pairs={{0,128},{128,0},{4,132},{132,4},{8,136},{136,8},{12,140},{140,12},... | collective-permute-start | bytes 15368 | tf_op jit(solution)/shard_map/ppermute | solution.py:19
  460.6 17.6 %collective-permute-start.1 = (f32[5,16,1,512]{3,1,2,0:T(8,128)}, f32[5,16,1,512]{3,1,2,0:T(8,128)S(1)}, u32[]{:S(2)}, u32[]{:S(2)}) collective-permute-start(f32[5,16,1,512]{3,1,2,0:T(8,128)} %get-tuple-element.12), channel_id=1, source_target_pairs={{4,0},{8,4},{12,8},{16,12},{20,16},{24,20},{28,24},{32,28},{36,32}... | collective-permute-start | bytes 491528 | tf_op jit(solution)/shard_map/ppermute | solution.py:32
  462.9 15.3 %collective-permute-start.2 = (f32[5,16,1,512]{3,1,2,0:T(8,128)}, f32[5,16,1,512]{3,1,2,0:T(8,128)}, u32[]{:S(2)}, u32[]{:S(2)}) collective-permute-start(f32[5,16,1,512]{3,1,2,0:T(8,128)} %get-tuple-element.11), channel_id=1, source_target_pairs={{0,4},{4,8},{8,12},{12,16},{16,20},{20,24},{24,28},{28,32},{32,36}... | collective-permute-start | bytes 491528 | tf_op jit(solution)/shard_map/ppermute | solution.py:29
  463.6 12.4 %collective-permute-start.3 = (f32[5,1,16,512]{3,2,1,0:T(8,128)}, f32[5,1,16,512]{3,2,1,0:T(8,128)}, u32[]{:S(2)}, u32[]{:S(2)}) collective-permute-start(f32[5,1,16,512]{3,2,1,0:T(8,128)} %copy.12), channel_id=1, source_target_pairs={{1,0},{2,1},{3,2},{5,4},{6,5},{7,6},{9,8},{10,9},{11,10},{13,12},{... | collective-permute-start | bytes 491528 | tf_op jit(solution)/shard_map/ppermute | solution.py:32
  470.2 6.9 %collective-permute-start.4 = (f32[5,1,16,512]{3,2,1,0:T(8,128)}, f32[5,1,16,512]{3,2,1,0:T(8,128)}, u32[]{:S(2)}, u32[]{:S(2)}) collective-permute-start(f32[5,1,16,512]{3,2,1,0:T(8,128)} %copy.14), channel_id=1, source_target_pairs={{0,1},{1,2},{2,3},{4,5},{5,6},{6,7},{8,9},{9,10},{10,11},{12,13},{... | collective-permute-start | bytes 491528 | tf_op jit(solution)/shard_map/ppermute | solution.py:29
Sparse Core Ops, SparseCore 0:
  10.8 363.8 all-gather.1
where the time goes:
time: 500 us; the launch traced here: 499 us
  waiting for transfers between devices  357 us (71%)
  matrix products  75.6 us (15%)
  other arithmetic  21.8 us (4%)
  local copies, waits for them, and re-layouts  17.6 us (4%)
  starting transfers between devices  13.9 us (3%)
  between operations  13.6 us (3%)
    all_gather x1, waiting for transfers between devices, on_device(): piece = lax.all_gather(inner_cycles, 'az', axis=2, tiled=True)  356 us
    dot_general x1, matrix products, on_device(): jnp.einsum('fztj,tc->fzjc', piece, piece_forward, precision=lax.Precision...  70.2 us
  transfers between devices with their start and end apart: 6, of which 2 were waited for; matrix products, arithmetic and copies ran while one was open for 3% of the time, Pallas kernels for 0%

commit v1 on v0

--- a/solution.py
+++ b/solution.py
@@ -82,7 +82,10 @@
     own_forward, own_inverse = mode_tables(own_index, total_theta, modes)
     inner_cycles = fields[:, :, :, :NEAR]
     kept = None
-    piece = lax.all_gather(inner_cycles, "az", axis=2, tiled=True)
+    n_dev = lax.axis_size("az")
+    blocks = jnp.stack([inner_cycles for _ in range(n_dev)])
+    blocks = lax.all_to_all(blocks, "az", split_axis=0, concat_axis=0)
+    piece = jnp.concatenate(blocks, axis=2)
     piece_index = jnp.arange(piece.shape[2], dtype=jnp.int32)
     piece_forward, unused_inverse = mode_tables(piece_index, total_theta, modes)
     spectra = jnp.einsum("fztj,tc->fzjc", piece, piece_forward, precision=lax.Precision.HIGHEST)

time: 500 us -> 642 us (1.28); the launches traced: 499 us -> 632 us
  local copies, waits for them, and re-layouts: 17.6 us -> 181 us
  waiting for transfers between devices: 357 us -> 273 us
  other arithmetic: 21.8 us -> 61.4 us
  starting transfers between devices: 13.9 us -> 40.3 us
  between operations: 13.6 us -> 0.43 us
    all_gather x1 -> x0, waiting for transfers between devices: 356 us -> none  [on_device(): piece = lax.all_gather(inner_cycles, 'az', axis=2, tiled=True)]
    all_to_all x0 -> x1, waiting for transfers between devices: none -> 273 us  [on_device(): blocks = lax.all_to_all(blocks, 'az', split_axis=0, concat_axis=0)]
    unnamed x3 -> x9, local copies, waits for them, and re-layouts: 3.25 us -> 126 us
    all_to_all x0 -> x1, other arithmetic: none -> 39.7 us  [on_device(): blocks = lax.all_to_all(blocks, 'az', split_axis=0, concat_axis=0)]
    reshape x0 -> x1, local copies, waits for them, and re-layouts: none -> 28.6 us  [on_device(): piece = jnp.concatenate(blocks, axis=2)]
    all_to_all x0 -> x1, starting transfers between devices: none -> 15.5 us  [on_device(): blocks = lax.all_to_all(blocks, 'az', split_axis=0, concat_axis=0)]
    another operation x0 -> x1, local copies, waits for them, and re-layouts: none -> 13.9 us  [on_device(): blocks = jnp.stack([inner_cycles for _ in range(n_dev)])]
    ppermute x2, starting transfers between devices: 8.24 us -> 19.3 us  [with_halo(): lax.ppermute(lax.slice_in_dim(block, 0, width, axis=dim), axis, backward)]
  transfers between devices with their start and end apart: 6 -> 6, of which waited for: 2 -> 1; matrix products, arithmetic and copies ran while one was open for 3% -> 2% of each run, Pallas kernels for 0% -> 0%
where the time goes in v1:
time: 642 us; the launch traced here: 632 us
  waiting for transfers between devices  273 us (43%)
  local copies, waits for them, and re-layouts  181 us (28%)
  matrix products  75.8 us (12%)
  other arithmetic  61.4 us (10%)
  starting transfers between devices  40.3 us (6%)
    all_to_all x1, waiting for transfers between devices, on_device(): blocks = lax.all_to_all(blocks, 'az', split_axis=0, concat_axis=0)  273 us
    unnamed x9, local copies, waits for them, and re-layouts  126 us
    dot_general x1, matrix products, on_device(): jnp.einsum('fztj,tc->fzjc', piece, piece_forward, precision=lax.Precision...  70.4 us
    all_to_all x1, other arithmetic, on_device(): blocks = lax.all_to_all(blocks, 'az', split_axis=0, concat_axis=0)  39.7 us
    reshape x1, local copies, waits for them, and re-layouts, on_device(): piece = jnp.concatenate(blocks, axis=2)  28.6 us
    ppermute x2, starting transfers between devices, with_halo(): lax.ppermute(lax.slice_in_dim(block, 0, width, axis=dim), axis, backward)  19.3 us
    all_to_all x1, starting transfers between devices, on_device(): blocks = lax.all_to_all(blocks, 'az', split_axis=0, concat_axis=0)  15.5 us
    another operation x1, local copies, waits for them, and re-layouts, on_device(): blocks = jnp.stack([inner_cycles for _ in range(n_dev)])  13.9 us
  transfers between devices with their start and end apart: 6, of which 1 were waited for; matrix products, arithmetic and copies ran while one was open for 2% of the time, Pallas kernels for 0%

profile of v1, /device:TPU:1, one launch (start us, length us, event | category | flops | bytes accessed | tf_op | source)
XLA Modules:
  0.0 632.3 jit_solution(12535912475822221283)
XLA Ops:
  0.0 1.1 slice.73
  1.1 13.9 %stack.2 = f32[64,5,16,16,40]{4,3,2,1,0:T(8,128)} broadcast(f32[5,16,16,40]{3,2,1,0:T(8,128)S(1)} %slice.73), dimensions={1,2,3,4} | broadcast | bytes 13312000 | tf_op jit(solution)/shard_map/stack | solution.py:86
  15.1 58.5 %reshape.66 = f32[64,1,51200]{2,1,0:T(1,128)} reshape(f32[64,5,16,16,40]{4,3,2,1,0:T(8,128)} %stack.2) | data formatting | bytes 26214400
  73.6 0.0 copy-start
  73.6 15.5 %all-to-all-start = ((f32[64,1,51200]{2,1,0:T(1,128)}), f32[64,1,51200]{2,1,0:T(1,128)}, u32[]{:S(2)}, u32[]{:S(2)}) async-start(f32[64,1,51200]{2,1,0:T(1,128)} %reshape.66), calls=%async_computation | async-start | bytes 26214400 | tf_op jit(solution)/shard_map/all_to_all | solution.py:87
  89.1 0.0 copy-done
  89.1 2.2 slice.74
  91.3 3.2 copy.24
  94.6 0.1 iota_compare_fusion
  94.7 0.1 fusion.43
  94.9 3.0 sine_multiply_fusion
  97.8 273.3 %all-to-all-done = f32[64,1,51200]{2,1,0:T(1,128)} async-done(((f32[64,1,51200]{2,1,0:T(1,128)}), f32[64,1,51200]{2,1,0:T(1,128)}, u32[]{:S(2)}, u32[]{:S(2)}) %all-to-all-start) | async-done | bytes 13107232 | tf_op jit(solution)/shard_map/all_to_all | solution.py:87
  371.1 0.6 broadcast.180
  371.7 39.7 %reduce.2 = f32[64,51200]{1,0:T(8,128)} reduce(f32[64,1,51200]{2,1,0:T(1,128)} %all-to-all-done, f32[]{:T(128)} %broadcast.180), dimensions={1}, to_apply=%all_to_all.3.reduce_sub_computation | reduce | bytes 26214404 | tf_op jit(solution)/shard_map/all_to_all | solution.py:87
  411.3 64.3 %reshape.67 = f32[64,5,16,16,40]{4,3,2,1,0:T(8,128)} reshape(f32[64,51200]{1,0:T(8,128)} %reduce.2) | data formatting | bytes 26214400
  475.7 28.6 %copy.11 = f32[5,16,64,16,40]{4,3,2,1,0:T(8,128)} copy(f32[5,16,64,16,40]{4,3,1,0,2:T(8,128)} %bitcast.29) | data formatting | bytes 26214400 | tf_op jit(solution)/shard_map/reshape | solution.py:88
  504.3 0.0 copy-done.1
  504.3 70.4 %fusion.8 = f32[256,5,16,40]{0,3,2,1:T(8,128)S(1)} fusion(f32[5,16,1024,40]{3,2,1,0:T(8,128)} %bitcast.28, f32[1024,128]{1,0:T(8,128)S(1)} %get-tuple-element.19, f32[1024,128]{1,0:T(8,128)S(1)} %copy-done.1), kind=kOutput, calls=%fused_computation.40 | convolution fusion | flops 10066591744 | bytes 17432576 | tf_op jit(solution)/shard_map/fztj,tc->fzjc/dot_general | solution.py:91
  574.7 5.4 fusion.7
  580.2 0.2 copy.14
  580.4 0.9 fusion.33
  581.3 4.0 fusion.1
  585.2 0.2 slice_reduce_fusion
  585.5 1.6 multiply_bitcast_fusion.1
  587.1 3.3 collective-permute-start
  590.4 0.7 fusion.31
  591.2 14.3 %collective-permute-start.1 = (f32[5,16,1,512]{3,1,2,0:T(8,128)}, f32[5,16,1,512]{3,1,2,0:T(8,128)S(1)}, u32[]{:S(2)}, u32[]{:S(2)}) collective-permute-start(f32[5,16,1,512]{3,1,2,0:T(8,128)} %get-tuple-element.12), channel_id=1, source_target_pairs={{4,0},{8,4},{12,8},{16,12},{20,16},{24,20},{28,24},{32,28},{36,32}... | collective-permute-start | bytes 491528 | tf_op jit(solution)/shard_map/ppermute | solution.py:32
  605.5 0.0 collective-permute-start.2
  605.5 0.7 copy.16
  606.2 4.9 collective-permute-start.3
  611.1 0.7 copy.18
  611.8 2.2 collective-permute-start.4
  614.0 0.0 collective-permute-done
  614.0 0.0 copy-done.2
  614.0 0.1 multiply_bitcast_fusion.2
  614.1 1.4 copy.15
  615.5 0.0 collective-permute-done.3
  615.5 1.1 copy.17
  616.6 0.0 collective-permute-done.4
  616.6 1.1 copy.19
  617.7 0.0 collective-permute-done.1
  617.7 0.0 collective-permute-done.2
  617.7 7.4 %multiply_add_fusion = f32[5,16,16,512]{3,1,2,0:T(8,128)S(1)} fusion(f32[5,1,16,512]{3,1,2,0:T(1,128)S(1)} %copy.17, f32[5,16,16,472]{3,1,2,0:T(8,128)S(1)} %copy.24, f32[5,16,16,40]{3,1,2,0:T(8,128)S(1)} %copy.14, f32[5,1,16,512]{3,1,2,0:T(1,128)S(1)} %copy.19, f32[5,16,16,511]{3,1,2,0:T(8,128)} %get-tuple-element.14, f32[5,16,16,1]{3,1,2,0:T(8,128)} %copy.15, ...), kind=kLoop, calls=%fused_computation.26 | loop fusion | flops 21626880 | bytes 12712960 | tf_op jit(solution)/shard_map/add | solution.py:118
  625.1 0.1 slice.122
  625.1 2.3 fusion.6
  627.4 0.8 fusion.26
  628.2 0.8 fusion.3
  629.1 3.0 copy.20
  (9 shorter events, 0.1 us)
Async XLA Ops:
  73.6 15.5 %copy-start = (f32[5,16,16,512]{3,2,1,0:T(8,128)S(1)}, f32[5,16,16,512]{3,2,1,0:T(8,128)}, u32[]{:S(2)}) copy-start(f32[5,16,16,512]{3,2,1,0:T(8,128)} %param.2) | copy-start | bytes 7864324
  73.6 297.5 %all-to-all-start = ((f32[64,1,51200]{2,1,0:T(1,128)}), f32[64,1,51200]{2,1,0:T(1,128)}, u32[]{:S(2)}, u32[]{:S(2)}) async-start(f32[64,1,51200]{2,1,0:T(1,128)} %reshape.66), calls=%async_computation | async-start | bytes 26214400 | tf_op jit(solution)/shard_map/all_to_all | solution.py:87
  475.7 28.6 %copy-start.1 = (f32[1024,128]{1,0:T(8,128)S(1)}, f32[1024,128]{1,0:T(8,128)}, u32[]{:S(2)}) copy-start(f32[1024,128]{1,0:T(8,128)} %get-tuple-element.20) | copy-start | bytes 1572868
  587.1 26.9 %copy-start.2 = (f32[5]{0:T(128)S(1)}, f32[5]{0:T(128)}, u32[]{:S(2)}) copy-start(f32[5]{0:T(128)} %constant.82.clone) | copy-start | bytes 64
  587.1 26.9 %collective-permute-start = (f32[5,16,16]{2,1,0:T(8,128)S(1)}, f32[5,16,16]{2,1,0:T(8,128)S(1)}, u32[]{:S(2)}, u32[]{:S(2)}) collective-permute-start(f32[5,16,16]{2,1,0:T(8,128)S(1)} %slice_reduce_fusion), channel_id=1, source_target_pairs={{0,128},{128,0},{4,132},{132,4},{8,136},{136,8},{12,140},{140,12},... | collective-permute-start | bytes 15368 | tf_op jit(solution)/shard_map/ppermute | solution.py:19
  591.2 26.5 %collective-permute-start.1 = (f32[5,16,1,512]{3,1,2,0:T(8,128)}, f32[5,16,1,512]{3,1,2,0:T(8,128)S(1)}, u32[]{:S(2)}, u32[]{:S(2)}) collective-permute-start(f32[5,16,1,512]{3,1,2,0:T(8,128)} %get-tuple-element.12), channel_id=1, source_target_pairs={{4,0},{8,4},{12,8},{16,12},{20,16},{24,20},{28,24},{32,28},{36,32}... | collective-permute-start | bytes 491528 | tf_op jit(solution)/shard_map/ppermute | solution.py:32
  605.5 12.2 %collective-permute-start.2 = (f32[5,16,1,512]{3,1,2,0:T(8,128)}, f32[5,16,1,512]{3,1,2,0:T(8,128)}, u32[]{:S(2)}, u32[]{:S(2)}) collective-permute-start(f32[5,16,1,512]{3,1,2,0:T(8,128)} %get-tuple-element.11), channel_id=1, source_target_pairs={{0,4},{4,8},{8,12},{12,16},{16,20},{20,24},{24,28},{28,32},{32,36}... | collective-permute-start | bytes 491528 | tf_op jit(solution)/shard_map/ppermute | solution.py:29
  606.2 9.3 %collective-permute-start.3 = (f32[5,1,16,512]{3,2,1,0:T(8,128)}, f32[5,1,16,512]{3,2,1,0:T(8,128)}, u32[]{:S(2)}, u32[]{:S(2)}) collective-permute-start(f32[5,1,16,512]{3,2,1,0:T(8,128)} %copy.16), channel_id=1, source_target_pairs={{1,0},{2,1},{3,2},{5,4},{6,5},{7,6},{9,8},{10,9},{11,10},{13,12},{... | collective-permute-start | bytes 491528 | tf_op jit(solution)/shard_map/ppermute | solution.py:32
  611.8 4.8 collective-permute-start.4
